TPU v7x, 256 devices: a whole 4x4x8 slice. The times are simulated.
256 devices in a mesh: src: 8 (over y, core), tgt: 32 (over z, x).
Axes of the slice: x: 4, y: 4, z: 8, core: 2. Of those that a mesh axis runs over, the one named last changes fastest.
Arguments:
- src_embed: bfloat16 [8192, 256], P('src'), may hold values from -128 to 128
- tgt_embed: bfloat16 [155648, 256], P('tgt'), may hold values from -1 to 1
- qwen_embed: bfloat16 [155648, 256], P('tgt'), may hold values from -6 to 6
- other_log: float32 [155648], P('tgt'), may hold values from -12 to -10
- src_counts: int32 [8192], P('src'), may hold values from 1 to 999
- tgt_counts: int32 [155648], P('tgt'), may hold values from 1 to 999
Outputs:
- transported: float32 [8192, 256], P(('src', 'tgt'))
All inputs are finite; a program needn't handle non-finite values.
Results may differ from a plain program's by a relative error of at most 0.0034.
Values sent between devices are 32-bit elements; how exact they have to be, the bound alone decides.
A program may use at most 128 MiB of HBM per device.

v0:
```python
import jax
import jax.numpy as jnp
from jax import lax
from jax.sharding import PartitionSpec as P

ITERS = 2
inv_temp = 4.0


def logits_of(src_embed, tgt_embed):
    products = lax.dot_general(
        src_embed, tgt_embed, (((1,), (1,)), ((), ())), preferred_element_type=jnp.float32
    )
    return products * inv_temp


def row_lse(values):
    local_peak = jnp.max(values, axis=1)
    peak = lax.pmax(local_peak, "tgt")
    total = lax.psum(jnp.sum(jnp.exp(values - peak[:, None]), axis=1), "tgt")
    return peak + jnp.log(total)


def col_lse(values):
    local_peak = jnp.max(values, axis=0)
    peak = lax.pmax(local_peak, "src")
    total = lax.psum(jnp.sum(jnp.exp(values - peak[None, :]), axis=0), "src")
    return peak + jnp.log(total)


def on_device(src_embed, tgt_embed, qwen_embed, other_log, src_counts, tgt_counts):
    src_float = src_counts.astype(jnp.float32)
    tgt_float = tgt_counts.astype(jnp.float32)
    slab_sum = lax.psum(jnp.sum(src_float), "src")
    vocab_sum = lax.psum(jnp.sum(tgt_float), "tgt")
    src_log = jnp.log(src_float) - jnp.log(slab_sum)
    tgt_log = jnp.log(tgt_float) - jnp.log(vocab_sum)
    stored = logits_of(src_embed, tgt_embed)

    def current():
        return stored

    col_pot = jnp.zeros((tgt_embed.shape[0],), jnp.float32)
    row_pot = jnp.zeros((src_embed.shape[0],), jnp.float32)
    for sweep in range(ITERS):
        row_pot = src_log - row_lse(current() + col_pot[None, :])
        col_pot = tgt_log - jnp.logaddexp(col_lse(current() + row_pot[:, None]), other_log)
    shift = row_pot - src_log
    weights = jnp.exp(shift[:, None] + col_pot[None, :] + current()).astype(jnp.bfloat16)
    owned_rows = src_embed.shape[0] // lax.axis_size("tgt")
    partial_rows = jnp.dot(weights, qwen_embed, preferred_element_type=jnp.float32)
    summed = lax.psum(partial_rows, "tgt")
    return lax.dynamic_slice_in_dim(summed, lax.axis_index("tgt") * owned_rows, owned_rows, 0)


def solution(mesh):
    return jax.shard_map(
        on_device,
        mesh=mesh,
        in_specs=(P("src", None), P("tgt", None), P("tgt", None), P("tgt"), P("src"), P("tgt")),
        out_specs=P(("src", "tgt"), None),
        check_vma=False,
    )
```

profile of v0, /device:TPU:8, one launch (start us, length us, event | category | flops | bytes accessed | tf_op | source)
XLA Modules:
  0.0 646.8 jit_solution(11345955397474943461)
XLA Ops:
  6.5 0.0 copy-start
  6.5 0.0 all-reduce.3.cloned.1.call-start
  6.5 1.5 convert_reduce_fusion
  8.0 1.3 convert_reduce_fusion.1
  9.3 0.0 copy-done
  9.3 0.0 copy-start.3
  9.3 9.3 %fusion.4 = (f32[1024]{0:T(1024)S(1)}, f32[1024,4864]{1,0:T(8,128)}) fusion(bf16[1024,256]{1,0:T(8,128)(2,1)} %param.6, bf16[4864,256]{1,0:T(8,128)(2,1)S(1)} %copy-done), kind=kOutput, calls=%fused_computation.24 | convolution fusion | flops 2560097280 | bytes 22941696 | tf_op jit(solution)/shard_map/dot_general | solution.py:11
  18.7 77.7 %pmax.28 = f32[1024]{0:T(1024)S(1)} all-reduce(f32[1024]{0:T(1024)S(1)} %get-tuple-element.9), channel_id=1, replica_groups=mesh['src'=8,'tgt'=32] {'tgt'}, use_global_device_ids=true, to_apply=%region_5.0 | all-reduce | flops 1024 | bytes 8192 | tf_op jit(solution)/shard_map/pmax | solution.py:19
  96.3 10.6 %psum.49 = f32[]{:T(128)} all-reduce(f32[]{:T(128)} %convert_reduce_fusion.1), channel_id=1, replica_groups=mesh['src'=8,'tgt'=32] {'src'}, use_global_device_ids=true, to_apply=%region_1.0 | all-reduce | flops 1 | bytes 8 | tf_op jit(solution)/shard_map/psum | solution.py:34
  107.7 9.4 %exponential_reduce_fusion.3 = f32[1024]{0:T(1024)S(1)} fusion(f32[1024,4864]{1,0:T(8,128)} %get-tuple-element.10, f32[1024]{0:T(1024)S(1)} %pmax.28), kind=kLoop, calls=%fused_computation.4 | loop fusion | flops 9960448 | bytes 19931136 | tf_op jit(solution)/shard_map/reduce_sum | solution.py:20
  117.1 71.1 %all-reduce = (f32[1024]{0:T(1024)S(1)}, f32[]{:T(128)}) all-reduce(f32[1024]{0:T(1024)S(1)} %exponential_reduce_fusion.3, f32[]{:T(128)} %convert_reduce_fusion), channel_id=1, replica_groups=mesh['src'=8,'tgt'=32] {'tgt'}, use_global_device_ids=true, to_apply=%region_7.0 | all-reduce | flops 1025 | bytes 8200 | tf_op jit(solution)/shard_map/psum | solution.py:20
  188.2 0.0 copy-done.3
  188.2 0.0 copy-start.1
  188.2 0.0 copy-start.2
  188.2 8.3 %add_reduce_fusion.2 = f32[4864]{0:T(1024)S(1)} fusion(f32[1024,4864]{1,0:T(8,128)} %get-tuple-element.10, f32[1024]{0:T(1024)S(1)} %add_subtract_fusion.1), kind=kLoop, calls=%fused_computation.7 | loop fusion | flops 9956608 | bytes 19946496 | tf_op jit(solution)/shard_map/reduce_max | solution.py:25
  196.5 23.0 %pmax.29 = f32[4864]{0:T(1024)S(1)} all-reduce(f32[4864]{0:T(1024)S(1)} %add_reduce_fusion.2), channel_id=1, replica_groups=mesh['src'=8,'tgt'=32] {'src'}, use_global_device_ids=true, to_apply=%region_9.0 | all-reduce | flops 4864 | bytes 38912 | tf_op jit(solution)/shard_map/pmax | solution.py:26
  219.5 10.9 %exponential_reduce_fusion.2 = f32[4864]{0:T(1024)S(1)} fusion(f32[1024,4864]{1,0:T(8,128)} %get-tuple-element.10, f32[4864]{0:T(1024)S(1)} %pmax.29, f32[1024]{0:T(1024)S(1)} %add_subtract_fusion.1), kind=kLoop, calls=%fused_computation.3 | loop fusion | flops 14937344 | bytes 19965952 | tf_op jit(solution)/shard_map/reduce_sum | solution.py:27
  230.4 23.8 %psum.52 = f32[4864]{0:T(1024)S(1)} all-reduce(f32[4864]{0:T(1024)S(1)} %exponential_reduce_fusion.2), channel_id=1, replica_groups=mesh['src'=8,'tgt'=32] {'src'}, use_global_device_ids=true, to_apply=%region_11.0 | all-reduce | flops 4864 | bytes 38912 | tf_op jit(solution)/shard_map/psum | solution.py:27
  254.9 0.0 copy-done.1
  254.9 0.0 copy-done.2
  254.9 8.1 %add_reduce_fusion.1 = f32[1024]{0:T(1024)S(1)} fusion(f32[1024,4864]{1,0:T(8,128)} %get-tuple-element.10, f32[4864]{0:T(1024)S(1)} %select_subtract_fusion.1), kind=kLoop, calls=%fused_computation.6 | loop fusion | flops 9960448 | bytes 19946496 | tf_op jit(solution)/shard_map/reduce_max | solution.py:18
  263.0 71.6 %pmax.30 = f32[1024]{0:T(1024)S(1)} all-reduce(f32[1024]{0:T(1024)S(1)} %add_reduce_fusion.1), channel_id=1, replica_groups=mesh['src'=8,'tgt'=32] {'tgt'}, use_global_device_ids=true, to_apply=%region_13.0 | all-reduce | flops 1024 | bytes 8192 | tf_op jit(solution)/shard_map/pmax | solution.py:19
  334.6 10.0 %exponential_reduce_fusion.1 = f32[1024]{0:T(1024)S(1)} fusion(f32[1024,4864]{1,0:T(8,128)} %get-tuple-element.10, f32[1024]{0:T(1024)S(1)} %pmax.30, f32[4864]{0:T(1024)S(1)} %select_subtract_fusion.1), kind=kLoop, calls=%fused_computation.2 | loop fusion | flops 14941184 | bytes 19950592 | tf_op jit(solution)/shard_map/reduce_sum | solution.py:20
  344.7 69.6 %psum.53 = f32[1024]{0:T(1024)S(1)} all-reduce(f32[1024]{0:T(1024)S(1)} %exponential_reduce_fusion.1), channel_id=1, replica_groups=mesh['src'=8,'tgt'=32] {'tgt'}, use_global_device_ids=true, to_apply=%region_15.0 | all-reduce | flops 1024 | bytes 8192 | tf_op jit(solution)/shard_map/psum | solution.py:20
  414.3 8.3 %add_reduce_fusion = f32[4864]{0:T(1024)S(1)} fusion(f32[1024,4864]{1,0:T(8,128)} %get-tuple-element.10, f32[1024]{0:T(1024)S(1)} %get-tuple-element.8), kind=kLoop, calls=%fused_computation.5 | loop fusion | flops 9956608 | bytes 19946496 | tf_op jit(solution)/shard_map/reduce_max | solution.py:25
  422.6 23.6 %pmax.31 = f32[4864]{0:T(1024)S(1)} all-reduce(f32[4864]{0:T(1024)S(1)} %add_reduce_fusion), channel_id=1, replica_groups=mesh['src'=8,'tgt'=32] {'src'}, use_global_device_ids=true, to_apply=%region_17.0 | all-reduce | flops 4864 | bytes 38912 | tf_op jit(solution)/shard_map/pmax | solution.py:26
  446.2 10.9 %exponential_reduce_fusion = f32[4864]{0:T(1024)S(1)} fusion(f32[1024,4864]{1,0:T(8,128)} %get-tuple-element.10, f32[4864]{0:T(1024)S(1)} %pmax.31, f32[1024]{0:T(1024)S(1)} %get-tuple-element.8), kind=kLoop, calls=%fused_computation.1 | loop fusion | flops 14937344 | bytes 19965952 | tf_op jit(solution)/shard_map/reduce_sum | solution.py:27
  457.1 23.8 %psum.54 = f32[4864]{0:T(1024)S(1)} all-reduce(f32[4864]{0:T(1024)S(1)} %exponential_reduce_fusion), channel_id=1, replica_groups=mesh['src'=8,'tgt'=32] {'src'}, use_global_device_ids=true, to_apply=%region_19.0 | all-reduce | flops 4864 | bytes 38912 | tf_op jit(solution)/shard_map/psum | solution.py:27
  480.9 11.5 %fusion = f32[1024,256]{1,0:T(8,128)} fusion(bf16[4864,256]{1,0:T(8,128)(2,1)} %param.8, f32[1024,4864]{1,0:T(8,128)} %get-tuple-element.10, f32[4864]{0:T(1024)S(1)} %select_subtract_fusion, f32[1024]{0:T(1024)S(1)} %get-tuple-element.7), kind=kOutput, calls=%fused_computation.9 | convolution fusion | flops 2565079040 | bytes 23485440 | tf_op jit(solution)/shard_map/dot_general | solution.py:51
  492.4 0.0 all-reduce.3.cloned.1.call-update
  492.5 146.1 %all-reduce.3.cloned.1.call-done = f32[1024,256]{1,0:T(8,128)} async-done(((f32[1024,256]{1,0:T(8,128)}), f32[1024,256]{1,0:T(8,128)}) %all-reduce.3.cloned.1.call-update) | async-done | bytes 1048592 | tf_op jit(solution)/shard_map/psum | solution.py:52
  638.6 1.4 constant_dynamic-slice_fusion
  (4 shorter events, 0.1 us)
Async XLA Ops:
  6.5 2.8 copy-start
  6.5 632.0 %all-reduce.3.cloned.1.call-start = ((), (), s32[]{:S(2)}) async-start(), calls=%async_computation | async-start | bytes 2097152 | tf_op jit(solution)/shard_map/psum | solution.py:52
  9.3 178.9 %copy-start.3 = (s32[1024]{0:T(1024)S(1)}, s32[1024]{0:T(1024)}, u32[]{:S(2)}) copy-start(s32[1024]{0:T(1024)} %param.10) | copy-start | bytes 12292
  188.2 66.7 %copy-start.1 = (s32[4864]{0:T(1024)S(1)}, s32[4864]{0:T(1024)}, u32[]{:S(2)}) copy-start(s32[4864]{0:T(1024)} %param.11) | copy-start | bytes 58372
  188.2 66.7 %copy-start.2 = (f32[4864]{0:T(1024)S(1)}, f32[4864]{0:T(1024)}, u32[]{:S(2)}) copy-start(f32[4864]{0:T(1024)} %param.9) | copy-start | bytes 58372
Sparse Core Ops, SparseCore 0:
  492.6 145.9 all-reduce.2
where the time goes:
time: 647 us
  blocking collectives  395 us (61%)
  waiting for transfers between devices  146 us (23%)
  other arithmetic  68.7 us (11%)
  matrix products  20.8 us (3%)
  between operations  14.8 us (2%)
    pmax x2, blocking collectives, row_lse(): peak = lax.pmax(local_peak, 'tgt')  149 us
    psum x1, waiting for transfers between devices, on_device(): summed = lax.psum(partial_rows, 'tgt')  146 us
    psum x2, blocking collectives, row_lse(): total = lax.psum(jnp.sum(jnp.exp(values - peak[:, None]), axis=1), 'tgt')  141 us
    psum x2, blocking collectives, col_lse(): total = lax.psum(jnp.sum(jnp.exp(values - peak[None, :]), axis=0), 'src')  47.6 us
    pmax x2, blocking collectives, col_lse(): peak = lax.pmax(local_peak, 'src')  46.6 us
    reduce_sum x2, other arithmetic, col_lse(): total = lax.psum(jnp.sum(jnp.exp(values - peak[None, :]), axis=0), 'src')  21.7 us
    reduce_sum x2, other arithmetic, row_lse(): total = lax.psum(jnp.sum(jnp.exp(values - peak[:, None]), axis=1), 'tgt')  19.4 us
    reduce_max x2, other arithmetic, col_lse(): local_peak = jnp.max(values, axis=0)  16.6 us
  transfers between devices with their start and end apart: 1, of which 1 were waited for; matrix products, arithmetic and copies ran while one was open for 0% of the time, Pallas kernels for 0%

commit v1 on v0

--- a/solution.py
+++ b/solution.py
@@ -5,6 +5,15 @@
 
 ITERS = 2
 inv_temp = 4.0
+
+
+def doubling_sum(x, axis):
+    peers = lax.axis_size(axis)
+    summed, stride = (x, 1)
+    while stride < peers:
+        summed = summed + lax.ppermute(summed, axis, [(i, i ^ stride) for i in range(peers)])
+        stride = 2 * stride
+    return summed
 
 
 def logits_of(src_embed, tgt_embed):
@@ -49,7 +58,7 @@
     weights = jnp.exp(shift[:, None] + col_pot[None, :] + current()).astype(jnp.bfloat16)
     owned_rows = src_embed.shape[0] // lax.axis_size("tgt")
     partial_rows = jnp.dot(weights, qwen_embed, preferred_element_type=jnp.float32)
-    summed = lax.psum(partial_rows, "tgt")
+    summed = doubling_sum(partial_rows, "tgt")
     return lax.dynamic_slice_in_dim(summed, lax.axis_index("tgt") * owned_rows, owned_rows, 0)
 
 

time: 647 us -> 677 us (1.046)
  the two profiles are of different devices: /device:TPU:8 before, /device:TPU:10 now
where the time goes in v1:
time: 677 us
  blocking collectives  395 us (58%)
  waiting for transfers between devices  190 us (28%)
  other arithmetic  70.6 us (10%)
  matrix products  18.5 us (3%)
    ppermute x5, waiting for transfers between devices, doubling_sum(): lax.ppermute(summed, axis, [(i, i ^ stride) for i in range(peers)])  190 us
    psum x2, blocking collectives, row_lse(): total = lax.psum(jnp.sum(jnp.exp(values - peak[:, None]), axis=1), 'tgt')  147 us
    pmax x2, blocking collectives, row_lse(): peak = lax.pmax(local_peak, 'tgt')  143 us
    psum x2, blocking collectives, col_lse(): total = lax.psum(jnp.sum(jnp.exp(values - peak[None, :]), axis=0), 'src')  47.6 us
    pmax x2, blocking collectives, col_lse(): peak = lax.pmax(local_peak, 'src')  46.5 us
    reduce_sum x2, other arithmetic, col_lse(): total = lax.psum(jnp.sum(jnp.exp(values - peak[None, :]), axis=0), 'src')  21.7 us
    reduce_sum x2, other arithmetic, row_lse(): total = lax.psum(jnp.sum(jnp.exp(values - peak[:, None]), axis=1), 'tgt')  19.4 us
    reduce_max x2, other arithmetic, col_lse(): local_peak = jnp.max(values, axis=0)  16.6 us
  transfers between devices with their start and end apart: 5, of which 5 were waited for; matrix products, arithmetic and copies ran while one was open for 0% of the time, Pallas kernels for 0%

profile of v1, /device:TPU:10, one launch (start us, length us, event | category | flops | bytes accessed | tf_op | source)
XLA Modules:
  0.0 676.5 jit_solution(12611341516364978688)
XLA Ops:
  0.0 0.0 copy-start
  0.0 1.5 convert_reduce_fusion
  1.5 1.3 convert_reduce_fusion.1
  2.8 0.0 copy-done
  2.8 0.0 copy-start.3
  2.8 9.3 %fusion.4 = (f32[1024]{0:T(1024)S(1)}, f32[1024,4864]{1,0:T(8,128)}) fusion(bf16[1024,256]{1,0:T(8,128)(2,1)} %param.6, bf16[4864,256]{1,0:T(8,128)(2,1)S(1)} %copy-done), kind=kOutput, calls=%fused_computation.24 | convolution fusion | flops 2560097280 | bytes 22941696 | tf_op jit(solution)/shard_map/dot_general | solution.py:20
  12.1 73.7 %pmax.28 = f32[1024]{0:T(1024)S(1)} all-reduce(f32[1024]{0:T(1024)S(1)} %get-tuple-element.9), channel_id=1, replica_groups=mesh['src'=8,'tgt'=32] {'tgt'}, use_global_device_ids=true, to_apply=%region_5.0 | all-reduce | flops 1024 | bytes 8192 | tf_op jit(solution)/shard_map/pmax | solution.py:28
  85.8 10.6 %psum.42 = f32[]{:T(128)} all-reduce(f32[]{:T(128)} %convert_reduce_fusion.1), channel_id=1, replica_groups=mesh['src'=8,'tgt'=32] {'src'}, use_global_device_ids=true, to_apply=%region_1.0 | all-reduce | flops 1 | bytes 8 | tf_op jit(solution)/shard_map/psum | solution.py:43
  97.1 9.4 %exponential_reduce_fusion.3 = f32[1024]{0:T(1024)S(1)} fusion(f32[1024,4864]{1,0:T(8,128)} %get-tuple-element.10, f32[1024]{0:T(1024)S(1)} %pmax.28), kind=kLoop, calls=%fused_computation.4 | loop fusion | flops 9960448 | bytes 19931136 | tf_op jit(solution)/shard_map/reduce_sum | solution.py:29
  106.5 75.7 %all-reduce = (f32[1024]{0:T(1024)S(1)}, f32[]{:T(128)}) all-reduce(f32[1024]{0:T(1024)S(1)} %exponential_reduce_fusion.3, f32[]{:T(128)} %convert_reduce_fusion), channel_id=1, replica_groups=mesh['src'=8,'tgt'=32] {'tgt'}, use_global_device_ids=true, to_apply=%region_7.0 | all-reduce | flops 1025 | bytes 8200 | tf_op jit(solution)/shard_map/psum | solution.py:29
  182.2 0.0 copy-done.3
  182.2 0.0 copy-start.1
  182.2 0.0 copy-start.2
  182.2 8.3 %add_reduce_fusion.2 = f32[4864]{0:T(1024)S(1)} fusion(f32[1024,4864]{1,0:T(8,128)} %get-tuple-element.10, f32[1024]{0:T(1024)S(1)} %add_subtract_fusion.1), kind=kLoop, calls=%fused_computation.7 | loop fusion | flops 9956608 | bytes 19946496 | tf_op jit(solution)/shard_map/reduce_max | solution.py:34
  190.5 23.0 %pmax.29 = f32[4864]{0:T(1024)S(1)} all-reduce(f32[4864]{0:T(1024)S(1)} %add_reduce_fusion.2), channel_id=1, replica_groups=mesh['src'=8,'tgt'=32] {'src'}, use_global_device_ids=true, to_apply=%region_9.0 | all-reduce | flops 4864 | bytes 38912 | tf_op jit(solution)/shard_map/pmax | solution.py:35
  213.5 10.9 %exponential_reduce_fusion.2 = f32[4864]{0:T(1024)S(1)} fusion(f32[1024,4864]{1,0:T(8,128)} %get-tuple-element.10, f32[4864]{0:T(1024)S(1)} %pmax.29, f32[1024]{0:T(1024)S(1)} %add_subtract_fusion.1), kind=kLoop, calls=%fused_computation.3 | loop fusion | flops 14937344 | bytes 19965952 | tf_op jit(solution)/shard_map/reduce_sum | solution.py:36
  224.4 23.8 %psum.45 = f32[4864]{0:T(1024)S(1)} all-reduce(f32[4864]{0:T(1024)S(1)} %exponential_reduce_fusion.2), channel_id=1, replica_groups=mesh['src'=8,'tgt'=32] {'src'}, use_global_device_ids=true, to_apply=%region_11.0 | all-reduce | flops 4864 | bytes 38912 | tf_op jit(solution)/shard_map/psum | solution.py:36
  248.8 0.0 copy-done.1
  248.8 0.0 copy-done.2
  248.9 8.1 %add_reduce_fusion.1 = f32[1024]{0:T(1024)S(1)} fusion(f32[1024,4864]{1,0:T(8,128)} %get-tuple-element.10, f32[4864]{0:T(1024)S(1)} %select_subtract_fusion.1), kind=kLoop, calls=%fused_computation.6 | loop fusion | flops 9960448 | bytes 19946496 | tf_op jit(solution)/shard_map/reduce_max | solution.py:27
  257.0 69.7 %pmax.30 = f32[1024]{0:T(1024)S(1)} all-reduce(f32[1024]{0:T(1024)S(1)} %add_reduce_fusion.1), channel_id=1, replica_groups=mesh['src'=8,'tgt'=32] {'tgt'}, use_global_device_ids=true, to_apply=%region_13.0 | all-reduce | flops 1024 | bytes 8192 | tf_op jit(solution)/shard_map/pmax | solution.py:28
  326.6 10.0 %exponential_reduce_fusion.1 = f32[1024]{0:T(1024)S(1)} fusion(f32[1024,4864]{1,0:T(8,128)} %get-tuple-element.10, f32[1024]{0:T(1024)S(1)} %pmax.30, f32[4864]{0:T(1024)S(1)} %select_subtract_fusion.1), kind=kLoop, calls=%fused_computation.2 | loop fusion | flops 14941184 | bytes 19950592 | tf_op jit(solution)/shard_map/reduce_sum | solution.py:29
  336.6 71.6 %psum.46 = f32[1024]{0:T(1024)S(1)} all-reduce(f32[1024]{0:T(1024)S(1)} %exponential_reduce_fusion.1), channel_id=1, replica_groups=mesh['src'=8,'tgt'=32] {'tgt'}, use_global_device_ids=true, to_apply=%region_15.0 | all-reduce | flops 1024 | bytes 8192 | tf_op jit(solution)/shard_map/psum | solution.py:29
  408.3 8.3 %add_reduce_fusion = f32[4864]{0:T(1024)S(1)} fusion(f32[1024,4864]{1,0:T(8,128)} %get-tuple-element.10, f32[1024]{0:T(1024)S(1)} %get-tuple-element.8), kind=kLoop, calls=%fused_computation.5 | loop fusion | flops 9956608 | bytes 19946496 | tf_op jit(solution)/shard_map/reduce_max | solution.py:34
  416.6 23.6 %pmax.31 = f32[4864]{0:T(1024)S(1)} all-reduce(f32[4864]{0:T(1024)S(1)} %add_reduce_fusion), channel_id=1, replica_groups=mesh['src'=8,'tgt'=32] {'src'}, use_global_device_ids=true, to_apply=%region_17.0 | all-reduce | flops 4864 | bytes 38912 | tf_op jit(solution)/shard_map/pmax | solution.py:35
  440.2 10.9 %exponential_reduce_fusion = f32[4864]{0:T(1024)S(1)} fusion(f32[1024,4864]{1,0:T(8,128)} %get-tuple-element.10, f32[4864]{0:T(1024)S(1)} %pmax.31, f32[1024]{0:T(1024)S(1)} %get-tuple-element.8), kind=kLoop, calls=%fused_computation.1 | loop fusion | flops 14937344 | bytes 19965952 | tf_op jit(solution)/shard_map/reduce_sum | solution.py:36
  451.0 23.8 %psum.47 = f32[4864]{0:T(1024)S(1)} all-reduce(f32[4864]{0:T(1024)S(1)} %exponential_reduce_fusion), channel_id=1, replica_groups=mesh['src'=8,'tgt'=32] {'src'}, use_global_device_ids=true, to_apply=%region_19.0 | all-reduce | flops 4864 | bytes 38912 | tf_op jit(solution)/shard_map/psum | solution.py:36
  474.9 9.1 %fusion = f32[1024,256]{1,0:T(8,128)S(1)} fusion(bf16[4864,256]{1,0:T(8,128)(2,1)} %param.8, f32[1024,4864]{1,0:T(8,128)} %get-tuple-element.10, f32[4864]{0:T(1024)S(1)} %select_subtract_fusion, f32[1024]{0:T(1024)S(1)} %get-tuple-element.7), kind=kOutput, calls=%fused_computation.9 | convolution fusion | flops 2565079040 | bytes 23485440 | tf_op jit(solution)/shard_map/dot_general | solution.py:60
  484.0 0.1 collective-permute-start
  484.1 24.3 %collective-permute-done = f32[1024,256]{1,0:T(8,128)S(1)} collective-permute-done((f32[1024,256]{1,0:T(8,128)S(1)}, f32[1024,256]{1,0:T(8,128)S(1)}, u32[]{:S(2)}, u32[]{:S(2)}) %collective-permute-start) | collective-permute-done | bytes 1048608 | tf_op jit(solution)/shard_map/ppermute | solution.py:14
  508.4 0.1 add.112
  508.5 0.1 collective-permute-start.1
  508.6 23.0 %collective-permute-done.1 = f32[1024,256]{1,0:T(8,128)S(1)} collective-permute-done((f32[1024,256]{1,0:T(8,128)S(1)}, f32[1024,256]{1,0:T(8,128)S(1)}, u32[]{:S(2)}, u32[]{:S(2)}) %collective-permute-start.1) | collective-permute-done | bytes 1048608 | tf_op jit(solution)/shard_map/ppermute | solution.py:14
  531.6 0.1 add.113
  531.7 0.1 collective-permute-start.2
  531.8 20.9 %collective-permute-done.2 = f32[1024,256]{1,0:T(8,128)S(1)} collective-permute-done((f32[1024,256]{1,0:T(8,128)S(1)}, f32[1024,256]{1,0:T(8,128)S(1)}, u32[]{:S(2)}, u32[]{:S(2)}) %collective-permute-start.2) | collective-permute-done | bytes 1048608 | tf_op jit(solution)/shard_map/ppermute | solution.py:14
  552.7 0.1 add.114
  552.9 0.1 collective-permute-start.3
  553.0 83.6 %collective-permute-done.3 = f32[1024,256]{1,0:T(8,128)S(1)} collective-permute-done((f32[1024,256]{1,0:T(8,128)S(1)}, f32[1024,256]{1,0:T(8,128)S(1)}, u32[]{:S(2)}, u32[]{:S(2)}) %collective-permute-start.3) | collective-permute-done | bytes 1048608 | tf_op jit(solution)/shard_map/ppermute | solution.py:14
  636.5 0.1 add.115
  636.7 0.1 collective-permute-start.4
  636.8 38.4 %collective-permute-done.4 = f32[1024,256]{1,0:T(8,128)} collective-permute-done((f32[1024,256]{1,0:T(8,128)S(1)}, f32[1024,256]{1,0:T(8,128)}, u32[]{:S(2)}, u32[]{:S(2)}) %collective-permute-start.4) | collective-permute-done | bytes 1048608 | tf_op jit(solution)/shard_map/ppermute | solution.py:14
  675.2 1.4 dynamic-slice_add_fusion
  (4 shorter events, 0.1 us)
Async XLA Ops:
  0.0 2.8 copy-start
  2.8 179.4 %copy-start.3 = (s32[1024]{0:T(1024)S(1)}, s32[1024]{0:T(1024)}, u32[]{:S(2)}) copy-start(s32[1024]{0:T(1024)} %param.10) | copy-start | bytes 12292
  182.2 66.6 %copy-start.1 = (s32[4864]{0:T(1024)S(1)}, s32[4864]{0:T(1024)}, u32[]{:S(2)}) copy-start(s32[4864]{0:T(1024)} %param.11) | copy-start | bytes 58372
  182.2 66.6 %copy-start.2 = (f32[4864]{0:T(1024)S(1)}, f32[4864]{0:T(1024)}, u32[]{:S(2)}) copy-start(f32[4864]{0:T(1024)} %param.9) | copy-start | bytes 58372
  484.0 24.4 %collective-permute-start = (f32[1024,256]{1,0:T(8,128)S(1)}, f32[1024,256]{1,0:T(8,128)S(1)}, u32[]{:S(2)}, u32[]{:S(2)}) collective-permute-start(f32[1024,256]{1,0:T(8,128)S(1)} %fusion), channel_id=1, source_target_pairs={{0,1},{1,0},{2,3},{3,2},{4,5},{5,4},{6,7},{7,6},{8,9},{9,8},{10,11... | collective-permute-start | bytes 3145736 | tf_op jit(solution)/shard_map/ppermute | solution.py:14
  508.5 23.1 %collective-permute-start.1 = (f32[1024,256]{1,0:T(8,128)S(1)}, f32[1024,256]{1,0:T(8,128)S(1)}, u32[]{:S(2)}, u32[]{:S(2)}) collective-permute-start(f32[1024,256]{1,0:T(8,128)S(1)} %add.112), channel_id=1, source_target_pairs={{0,2},{1,3},{2,0},{3,1},{4,6},{5,7},{6,4},{7,5},{8,10},{9,11},{10,... | collective-permute-start | bytes 3145736 | tf_op jit(solution)/shard_map/ppermute | solution.py:14
  531.7 21.0 %collective-permute-start.2 = (f32[1024,256]{1,0:T(8,128)S(1)}, f32[1024,256]{1,0:T(8,128)S(1)}, u32[]{:S(2)}, u32[]{:S(2)}) collective-permute-start(f32[1024,256]{1,0:T(8,128)S(1)} %add.113), channel_id=1, source_target_pairs={{0,4},{1,5},{2,6},{3,7},{4,0},{5,1},{6,2},{7,3},{8,12},{9,13},{10,... | collective-permute-start | bytes 3145736 | tf_op jit(solution)/shard_map/ppermute | solution.py:14
  552.9 83.7 %collective-permute-start.3 = (f32[1024,256]{1,0:T(8,128)S(1)}, f32[1024,256]{1,0:T(8,128)S(1)}, u32[]{:S(2)}, u32[]{:S(2)}) collective-permute-start(f32[1024,256]{1,0:T(8,128)S(1)} %add.114), channel_id=1, source_target_pairs={{0,8},{1,9},{2,10},{3,11},{4,12},{5,13},{6,14},{7,15},{8,0},{9,1},... | collective-permute-start | bytes 3145736 | tf_op jit(solution)/shard_map/ppermute | solution.py:14
  636.7 38.5 %collective-permute-start.4 = (f32[1024,256]{1,0:T(8,128)S(1)}, f32[1024,256]{1,0:T(8,128)}, u32[]{:S(2)}, u32[]{:S(2)}) collective-permute-start(f32[1024,256]{1,0:T(8,128)S(1)} %add.115), channel_id=1, source_target_pairs={{0,16},{1,17},{2,18},{3,19},{4,20},{5,21},{6,22},{7,23},{8,24},{9,... | collective-permute-start | bytes 3145736 | tf_op jit(solution)/shard_map/ppermute | solution.py:14
